TPU v7x, 128 devices: a whole 4x4x4 slice. The times are simulated.
128 devices in a mesh: orbit: 32 (over y, z, core), region: 4 (over x).
Axes of the slice: x: 4, y: 4, z: 4, core: 2. Of those that a mesh axis runs over, the one named last changes fastest.
Arguments:
- footprints: bfloat16 [40960, 64, 256], P(('orbit', 'region')), may hold values from -0.0625 to 0.0625
- block_sounding: int32 [40960], P(('orbit', 'region')), may hold values from 0 to 31
- block_tile: int32 [40960], P(('orbit', 'region')), may hold values from 0 to 31
- block_count: int32 [128], P(('orbit', 'region')), may hold values from 80 to 320, as said below
- observations: float32 [1024, 64, 128], P('orbit'), may hold values from -6 to 6
- obs_weight: float32 [1024, 64], P('orbit'), may hold values from 0.25 to 4
- prior_std: float32 [4, 32, 256], P('region', 'orbit'), may hold values from 0.4 to 4.8
Outputs:
- flux: float32 [4, 32, 256, 128], P('region', 'orbit')
- residual: float32 [4, 32, 256, 128], P('region', 'orbit')
Inputs may be any that keep to these rules, and one draw needn't show every extreme that they name: `block_sounding`: index of a sounding block among the 32 of the block's orbit index. `block_tile`: index of a tile among the 32 of the block's region; some tiles are named far more often than others. `block_count`: slots from this count on are unused; some device has all 320 slots live.
All inputs are finite; a program needn't handle non-finite values.
Results may differ from a plain program's by a relative error of at most 0.0068.
Values may be sent and summed in bfloat16 or wider, within the bound.
A program may use at most 128 MiB of HBM per device.

v0:
```python
import jax
import jax.numpy as jnp
from jax import lax
from jax.sharding import PartitionSpec as P

ITERS = 2
GROUP = 64


def local_forward(footprints, block_sounding, block_tile, live_count, whole, sb_count):
    rounds = (live_count + GROUP - 1) // GROUP
    positions = jnp.arange(GROUP, dtype=jnp.int32)
    width = whole.shape[2]

    def turn(turn_index, running):
        offset = turn_index * GROUP
        blocks_now = lax.dynamic_slice_in_dim(footprints, offset, GROUP, 0)
        sound_ids = lax.dynamic_slice_in_dim(block_sounding, offset, GROUP, 0)
        tile_ids = lax.dynamic_slice_in_dim(block_tile, offset, GROUP, 0)
        alive = offset + positions < live_count
        targets = jnp.where(alive, sound_ids, sb_count)
        products = jnp.einsum(
            "bsc,bcr->bsr", blocks_now, whole[tile_ids], preferred_element_type=jnp.float32
        )
        return running + jax.ops.segment_sum(products, targets, num_segments=sb_count)

    start_sum = jnp.zeros((sb_count, footprints.shape[1], width), jnp.float32)
    return lax.fori_loop(0, rounds, turn, start_sum)


def local_transpose(footprints, block_sounding, block_tile, live_count, weighted, tile_count):
    rounds = (live_count + GROUP - 1) // GROUP
    positions = jnp.arange(GROUP, dtype=jnp.int32)
    width = weighted.shape[2]

    def turn(turn_index, running):
        offset = turn_index * GROUP
        blocks_now = lax.dynamic_slice_in_dim(footprints, offset, GROUP, 0)
        sound_ids = lax.dynamic_slice_in_dim(block_sounding, offset, GROUP, 0)
        tile_ids = lax.dynamic_slice_in_dim(block_tile, offset, GROUP, 0)
        alive = offset + positions < live_count
        targets = jnp.where(alive, tile_ids, tile_count)
        contrib = jnp.einsum(
            "bsc,bsr->bcr", blocks_now, weighted[sound_ids], preferred_element_type=jnp.float32
        )
        return running + jax.ops.segment_sum(contrib, targets, num_segments=tile_count)

    start_sum = jnp.zeros((tile_count, footprints.shape[2], width), jnp.float32)
    return lax.fori_loop(0, rounds, turn, start_sum)


def per_device(
    footprints, block_sounding, block_tile, block_count, observations, obs_weight, prior_std
):
    live_count = block_count[0]
    share_rows = prior_std.shape[1]
    tile_count = share_rows * lax.axis_size("orbit")
    sb_count = observations.shape[0]
    weight = obs_weight[:, :, None]
    prior_scale = prior_std[0][:, :, None]

    def reduce_tiles(partial_value):
        return lax.psum_scatter(partial_value, "orbit", scatter_dimension=0, tiled=True)

    def inner_sum(first_vec, second_vec):
        return lax.psum(jnp.sum(first_vec * second_vec, axis=(0, 1)), ("orbit", "region"))

    def apply_transpose(weighted):
        return reduce_tiles(
            local_transpose(
                footprints, block_sounding, block_tile, live_count, weighted, tile_count
            )
        )

    weighted0 = (weight * observations).astype(jnp.bfloat16)
    right_side = prior_scale * apply_transpose(weighted0)
    iterate = jnp.zeros_like(right_side)
    residual = right_side
    direction = right_side
    norm_now = inner_sum(residual, residual)
    for iteration in range(ITERS):
        scaled = (prior_scale * direction).astype(jnp.bfloat16)
        partial_value = local_forward(
            footprints,
            block_sounding,
            block_tile,
            live_count,
            lax.all_gather(scaled, "orbit", axis=0, tiled=True),
            sb_count,
        )
        image = lax.psum(partial_value, "region")
        weighted = (weight * image).astype(jnp.bfloat16)
        product = direction + prior_scale * apply_transpose(weighted)
        step_size = norm_now / inner_sum(direction, product)
        iterate = iterate + step_size * direction
        residual = residual - step_size * product
        if iteration + 1 < ITERS:
            norm_next = inner_sum(residual, residual)
            direction = residual + norm_next / norm_now * direction
            norm_now = norm_next
    flux = prior_scale * iterate
    return (flux[None], residual[None])


def solution(mesh):
    return jax.shard_map(
        per_device,
        mesh=mesh,
        in_specs=(
            P(("orbit", "region"), None, None),
            P(("orbit", "region")),
            P(("orbit", "region")),
            P(("orbit", "region")),
            P("orbit", None, None),
            P("orbit", None),
            P("region", "orbit", None),
        ),
        out_specs=(P("region", "orbit", None, None), P("region", "orbit", None, None)),
        check_vma=False,
    )
```

profile of v0, /device:TPU:1, one launch (start us, length us, event | category | flops | bytes accessed | tf_op | source)
XLA Modules:
  0.0 1179.8 jit_solution(10084983206093327789)
XLA Ops:
  9.5 2.5 broadcast.40.clone.1
  11.9 106.8 %while.55 = (s32[]{:T(128)}, f32[32,256,128]{2,1,0:T(8,128)}, s32[]{:T(128)}, s32[]{:T(128)}, s32[320]{0:T(512)S(1)}, /*index=5*/bf16[320,64,256]{2,1,0:T(8,128)...) while((s32[]{:T(128)}, f32[32,256,128]{2,1,0:T(8,128)}, ...), condition=%wide.region_2.3_spmd.clone, body=%wide.region_0.2_spmd.clone.sunk | while | flops 270534016 | bytes 38803376 | solution.py:49
  13.4 6.1 fusion.47
  19.5 19.0 %scatter_fusion = f32[32,256,128]{2,1,0:T(8,128)} fusion(f32[32,256,128]{2,1,0:T(8,128)} %get-tuple-element.721, s32[64]{0:T(128)S(1)} %get-tuple-element.666, f32[64,256,128]{2,1,0:T(8,128)} %fusion.47), kind=kCustom, calls=%fused_computation.5.clone.clone.1 | custom fusion | flops 2097152 | bytes 25166080 | tf_op jit(solution)/shard_map/while/body/scatter-add | solution.py:46
  40.1 6.1 fusion.47
  46.2 18.9 %scatter_fusion = f32[32,256,128]{2,1,0:T(8,128)} fusion(f32[32,256,128]{2,1,0:T(8,128)} %get-tuple-element.721, s32[64]{0:T(128)S(1)} %get-tuple-element.666, f32[64,256,128]{2,1,0:T(8,128)} %fusion.47), kind=kCustom, calls=%fused_computation.5.clone.clone.1 | custom fusion | flops 2097152 | bytes 25166080 | tf_op jit(solution)/shard_map/while/body/scatter-add | solution.py:46
  66.6 6.1 fusion.47
  72.7 19.0 %scatter_fusion = f32[32,256,128]{2,1,0:T(8,128)} fusion(f32[32,256,128]{2,1,0:T(8,128)} %get-tuple-element.721, s32[64]{0:T(128)S(1)} %get-tuple-element.666, f32[64,256,128]{2,1,0:T(8,128)} %fusion.47), kind=kCustom, calls=%fused_computation.5.clone.clone.1 | custom fusion | flops 2097152 | bytes 25166080 | tf_op jit(solution)/shard_map/while/body/scatter-add | solution.py:46
  93.2 6.1 fusion.47
  99.3 19.4 %scatter_fusion = f32[32,256,128]{2,1,0:T(8,128)} fusion(f32[32,256,128]{2,1,0:T(8,128)} %get-tuple-element.721, s32[64]{0:T(128)S(1)} %get-tuple-element.666, f32[64,256,128]{2,1,0:T(8,128)} %fusion.47), kind=kCustom, calls=%fused_computation.5.clone.clone.1 | custom fusion | flops 2097152 | bytes 25166080 | tf_op jit(solution)/shard_map/while/body/scatter-add | solution.py:46
  118.8 109.6 %reduce-scatter.4.cloned.1.call-done = f32[1,256,128]{2,1,0:T(8,128)} async-done(((f32[32,256,128]{2,1,0:T(8,128)}), f32[1,256,128]{2,1,0:T(8,128)}) %reduce-scatter.4.cloned.1.call-update) | async-done | bytes 131088 | tf_op jit(solution)/shard_map/reduce_scatter | solution.py:63
  230.2 46.2 %all-gather.3.cloned.1.call-done = bf16[32,256,128]{2,1,0:T(8,128)(2,1)} async-done(((bf16[1,256,128]{2,1,0:T(8,128)(2,1)}), bf16[32,256,128]{2,1,0:T(8,128)(2,1)}) %all-gather.3.cloned.1.call-update) | async-done | bytes 2097168 | tf_op jit(solution)/shard_map/all_gather | solution.py:88
  276.5 51.1 %while.56 = (s32[]{:T(128)}, f32[32,64,128]{2,1,0:T(8,128)S(1)}, s32[]{:T(128)}, s32[]{:T(128)}, s32[320]{0:T(512)S(1)}, /*index=5*/bf16[320,64,256]{2,1,0:T(8,1...) while((s32[]{:T(128)}, f32[32,64,128]{2,1,0:T(8,128)S(1)}, ...), condition=%wide.region_8.9_spmd.clone, body=%wide.region_6.8_spmd.clone.sunk | while | flops 268961152 | bytes 23074740 | solution.py:28
  277.3 4.6 gather_fusion.1
  281.9 3.7 fusion.50
  285.6 3.7 scatter_fusion.1
  290.1 4.6 gather_fusion.1
  294.7 3.7 fusion.50
  298.3 3.7 scatter_fusion.1
  302.8 4.6 gather_fusion.1
  307.4 3.7 fusion.50
  311.1 3.7 scatter_fusion.1
  315.6 4.6 gather_fusion.1
  320.2 3.7 fusion.50
  323.9 3.7 scatter_fusion.1
  328.7 55.4 %all-reduce.4.cloned.1.call-done = f32[32,64,128]{2,1,0:T(8,128)} async-done(((f32[32,64,128]{2,1,0:T(8,128)}), f32[32,64,128]{2,1,0:T(8,128)}) %all-reduce.4.cloned.1.call-update) | async-done | bytes 1048592 | tf_op jit(solution)/shard_map/psum | solution.py:91
  388.2 106.8 %while.57 = (s32[]{:T(128)}, f32[32,256,128]{2,1,0:T(8,128)}, s32[]{:T(128)}, s32[]{:T(128)}, s32[320]{0:T(512)S(1)}, /*index=5*/bf16[320,64,256]{2,1,0:T(8,128)...) while((s32[]{:T(128)}, f32[32,256,128]{2,1,0:T(8,128)}, ...), condition=%wide.region_12.13_spmd.clone, body=%wide.region_10.12_spmd.clone.sunk | while | flops 270534016 | bytes 38803376 | solution.py:49
  389.6 6.1 fusion.53
  395.8 19.0 %scatter_fusion.2 = f32[32,256,128]{2,1,0:T(8,128)} fusion(f32[32,256,128]{2,1,0:T(8,128)} %get-tuple-element.793, s32[64]{0:T(128)S(1)} %get-tuple-element.686, f32[64,256,128]{2,1,0:T(8,128)} %fusion.53), kind=kCustom, calls=%fused_computation.7.clone.clone.1 | custom fusion | flops 2097152 | bytes 25166080 | tf_op jit(solution)/shard_map/while/body/scatter-add | solution.py:46
  416.3 6.1 fusion.53
  422.4 18.9 %scatter_fusion.2 = f32[32,256,128]{2,1,0:T(8,128)} fusion(f32[32,256,128]{2,1,0:T(8,128)} %get-tuple-element.793, s32[64]{0:T(128)S(1)} %get-tuple-element.686, f32[64,256,128]{2,1,0:T(8,128)} %fusion.53), kind=kCustom, calls=%fused_computation.7.clone.clone.1 | custom fusion | flops 2097152 | bytes 25166080 | tf_op jit(solution)/shard_map/while/body/scatter-add | solution.py:46
  442.8 6.1 fusion.53
  448.9 19.0 %scatter_fusion.2 = f32[32,256,128]{2,1,0:T(8,128)} fusion(f32[32,256,128]{2,1,0:T(8,128)} %get-tuple-element.793, s32[64]{0:T(128)S(1)} %get-tuple-element.686, f32[64,256,128]{2,1,0:T(8,128)} %fusion.53), kind=kCustom, calls=%fused_computation.7.clone.clone.1 | custom fusion | flops 2097152 | bytes 25166080 | tf_op jit(solution)/shard_map/while/body/scatter-add | solution.py:46
  469.4 6.1 fusion.53
  475.5 19.4 %scatter_fusion.2 = f32[32,256,128]{2,1,0:T(8,128)} fusion(f32[32,256,128]{2,1,0:T(8,128)} %get-tuple-element.793, s32[64]{0:T(128)S(1)} %get-tuple-element.686, f32[64,256,128]{2,1,0:T(8,128)} %fusion.53), kind=kCustom, calls=%fused_computation.7.clone.clone.1 | custom fusion | flops 2097152 | bytes 25166080 | tf_op jit(solution)/shard_map/while/body/scatter-add | solution.py:46
  495.0 108.4 %reduce-scatter.6.cloned.1.call-done = f32[1,256,128]{2,1,0:T(8,128)} async-done(((f32[32,256,128]{2,1,0:T(8,128)}), f32[1,256,128]{2,1,0:T(8,128)}) %reduce-scatter.6.cloned.1.call-update) | async-done | bytes 131088 | tf_op jit(solution)/shard_map/reduce_scatter | solution.py:63
  604.4 65.9 %all-reduce = (f32[128]{0:T(128)S(1)}, f32[128]{0:T(128)S(1)}) all-reduce(f32[128]{0:T(128)S(1)} %get-tuple-element.343, f32[128]{0:T(128)S(1)} %get-tuple-element.342), channel_id=1, replica_groups=mesh['orbit'=32,'region'=4] {'orbit','region'}, use_global_device_ids=true, to_apply=%region_5.6 | all-reduce | flops 256 | bytes 2048 | tf_op jit(solution)/shard_map/psum | solution.py:66
  671.4 62.7 %psum.45 = f32[128]{0:T(128)S(1)} all-reduce(f32[128]{0:T(128)S(1)} %multiply_reduce_fusion.1), channel_id=1, replica_groups=mesh['orbit'=32,'region'=4] {'orbit','region'}, use_global_device_ids=true, to_apply=%region_17.18 | all-reduce | flops 128 | bytes 1024 | tf_op jit(solution)/shard_map/psum | solution.py:66
  735.8 41.3 %all-gather.5.cloned.1.call-done = bf16[32,256,128]{2,1,0:T(8,128)(2,1)} async-done(((bf16[1,256,128]{2,1,0:T(8,128)(2,1)}), bf16[32,256,128]{2,1,0:T(8,128)(2,1)}) %all-gather.5.cloned.1.call-update) | async-done | bytes 2097168 | tf_op jit(solution)/shard_map/all_gather | solution.py:88
  777.2 51.1 %while.58 = (s32[]{:T(128)}, f32[32,64,128]{2,1,0:T(8,128)S(1)}, s32[]{:T(128)}, s32[]{:T(128)}, s32[320]{0:T(512)S(1)}, /*index=5*/bf16[320,64,256]{2,1,0:T(8,1...) while((s32[]{:T(128)}, f32[32,64,128]{2,1,0:T(8,128)S(1)}, ...), condition=%wide.region_20.21_spmd.clone, body=%wide.region_18.20_spmd.clone.sunk | while | flops 268961152 | bytes 23074740 | solution.py:28
  778.0 4.6 gather_fusion.3
  782.6 3.7 fusion.56
  786.3 3.7 scatter_fusion.3
  790.7 4.6 gather_fusion.3
  795.3 3.7 fusion.56
  799.0 3.7 scatter_fusion.3
  803.5 4.6 gather_fusion.3
  808.1 3.7 fusion.56
  811.8 3.7 scatter_fusion.3
  816.3 4.6 gather_fusion.3
  820.9 3.7 fusion.56
  824.6 3.7 scatter_fusion.3
  829.4 55.4 %all-reduce.6.cloned.1.call-done = f32[32,64,128]{2,1,0:T(8,128)} async-done(((f32[32,64,128]{2,1,0:T(8,128)}), f32[32,64,128]{2,1,0:T(8,128)}) %all-reduce.6.cloned.1.call-update) | async-done | bytes 1048592 | tf_op jit(solution)/shard_map/psum | solution.py:91
  888.9 106.8 %while.59 = (s32[]{:T(128)}, f32[32,256,128]{2,1,0:T(8,128)}, s32[]{:T(128)}, s32[]{:T(128)}, s32[320]{0:T(512)S(1)}, /*index=5*/bf16[320,64,256]{2,1,0:T(8,128)...) while((s32[]{:T(128)}, f32[32,256,128]{2,1,0:T(8,128)}, ...), condition=%wide.region_24.25_spmd.clone, body=%wide.region_22.24_spmd.clone.sunk | while | flops 270534016 | bytes 38803376 | solution.py:49
  890.4 6.1 fusion.59
  896.5 19.0 %scatter_fusion.4 = f32[32,256,128]{2,1,0:T(8,128)} fusion(f32[32,256,128]{2,1,0:T(8,128)} %get-tuple-element.865, s32[64]{0:T(128)S(1)} %get-tuple-element.706, f32[64,256,128]{2,1,0:T(8,128)} %fusion.59), kind=kCustom, calls=%fused_computation.9.clone.clone.1 | custom fusion | flops 2097152 | bytes 25166080 | tf_op jit(solution)/shard_map/while/body/scatter-add | solution.py:46
  917.0 6.1 fusion.59
  923.1 18.9 %scatter_fusion.4 = f32[32,256,128]{2,1,0:T(8,128)} fusion(f32[32,256,128]{2,1,0:T(8,128)} %get-tuple-element.865, s32[64]{0:T(128)S(1)} %get-tuple-element.706, f32[64,256,128]{2,1,0:T(8,128)} %fusion.59), kind=kCustom, calls=%fused_computation.9.clone.clone.1 | custom fusion | flops 2097152 | bytes 25166080 | tf_op jit(solution)/shard_map/while/body/scatter-add | solution.py:46
  943.5 6.1 fusion.59
  949.6 19.0 %scatter_fusion.4 = f32[32,256,128]{2,1,0:T(8,128)} fusion(f32[32,256,128]{2,1,0:T(8,128)} %get-tuple-element.865, s32[64]{0:T(128)S(1)} %get-tuple-element.706, f32[64,256,128]{2,1,0:T(8,128)} %fusion.59), kind=kCustom, calls=%fused_computation.9.clone.clone.1 | custom fusion | flops 2097152 | bytes 25166080 | tf_op jit(solution)/shard_map/while/body/scatter-add | solution.py:46
  970.1 6.1 fusion.59
  976.3 19.4 %scatter_fusion.4 = f32[32,256,128]{2,1,0:T(8,128)} fusion(f32[32,256,128]{2,1,0:T(8,128)} %get-tuple-element.865, s32[64]{0:T(128)S(1)} %get-tuple-element.706, f32[64,256,128]{2,1,0:T(8,128)} %fusion.59), kind=kCustom, calls=%fused_computation.9.clone.clone.1 | custom fusion | flops 2097152 | bytes 25166080 | tf_op jit(solution)/shard_map/while/body/scatter-add | solution.py:46
  995.7 108.5 %reduce-scatter.8.cloned.1.call-done = f32[1,256,128]{2,1,0:T(8,128)} async-done(((f32[32,256,128]{2,1,0:T(8,128)}), f32[1,256,128]{2,1,0:T(8,128)}) %reduce-scatter.8.cloned.1.call-update) | async-done | bytes 131088 | tf_op jit(solution)/shard_map/reduce_scatter | solution.py:63
  1105.3 65.9 %psum.47 = f32[128]{0:T(128)S(1)} all-reduce(f32[128]{0:T(128)S(1)} %multiply_reduce_fusion), channel_id=1, replica_groups=mesh['orbit'=32,'region'=4] {'orbit','region'}, use_global_device_ids=true, to_apply=%region_27.28 | all-reduce | flops 128 | bytes 1024 | tf_op jit(solution)/shard_map/psum | solution.py:66
  (98 shorter events, 44.0 us)
Async XLA Ops:
  7.2 4.8 copy-start.6
  7.2 4.8 copy-start.5
  7.2 221.3 %reduce-scatter.4.cloned.1.call-start = ((), (), s32[]{:S(2)}) async-start(), calls=%async_computation.3 | async-start | bytes 4325376 | tf_op jit(solution)/shard_map/reduce_scatter | solution.py:63
  118.7 109.7 %copy-start.7 = (f32[1,1,256]{2,1,0:T(1,128)S(1)}, f32[1,1,256]{2,1,0:T(1,128)}, u32[]{:S(2)}) copy-start(f32[1,1,256]{2,1,0:T(1,128)} %param.23) | copy-start | bytes 3076
  118.7 157.7 %all-gather.3.cloned.1.call-start = ((), (), s32[]{:S(2)}) async-start(), calls=%async_computation.4 | async-start | bytes 2162688 | tf_op jit(solution)/shard_map/all_gather | solution.py:88
  230.1 154.0 %all-reduce.4.cloned.1.call-start = ((), (), s32[]{:S(2)}) async-start(), calls=%async_computation.5 | async-start | bytes 2097152 | tf_op jit(solution)/shard_map/psum | solution.py:91
  276.5 107.6 %copy-start.4 = (f32[32,64]{1,0:T(8,128)S(1)}, f32[32,64]{1,0:T(8,128)}, u32[]{:S(2)}) copy-start(f32[32,64]{1,0:T(8,128)} %param.22) | copy-start | bytes 24580
  327.6 1.0 copy-start
  328.7 274.7 %reduce-scatter.6.cloned.1.call-start = ((), (), s32[]{:S(2)}) async-start(), calls=%async_computation.6 | async-start | bytes 4325376 | tf_op jit(solution)/shard_map/reduce_scatter | solution.py:63
  495.0 108.5 %copy-start.2 = (f32[1,256,128]{2,1,0:T(8,128)S(1)}, f32[1,256,128]{2,1,0:T(8,128)}, u32[]{:S(2)}) copy-start(f32[1,256,128]{2,1,0:T(8,128)} %reduce-scatter.4.cloned.1.call-done) | copy-start | bytes 393220
  495.0 282.1 %all-gather.5.cloned.1.call-start = ((), (), s32[]{:S(2)}) async-start(), calls=%async_computation.7 | async-start | bytes 2162688 | tf_op jit(solution)/shard_map/all_gather | solution.py:88
  735.7 149.1 %all-reduce.6.cloned.1.call-start = ((), (), s32[]{:S(2)}) async-start(), calls=%async_computation.8 | async-start | bytes 2097152 | tf_op jit(solution)/shard_map/psum | solution.py:91
  828.3 1.0 copy-start.1
  829.4 274.9 %reduce-scatter.8.cloned.1.call-start = ((), (), s32[]{:S(2)}) async-start(), calls=%async_computation.9 | async-start | bytes 4325376 | tf_op jit(solution)/shard_map/reduce_scatter | solution.py:63
  995.7 108.6 %copy-start.3 = (f32[1,256,128]{2,1,0:T(8,128)S(1)}, f32[1,256,128]{2,1,0:T(8,128)}, u32[]{:S(2)}) copy-start(f32[1,256,128]{2,1,0:T(8,128)} %reduce-scatter.6.cloned.1.call-done) | copy-start | bytes 393220
Sparse Core Ops, SparseCore 0:
  118.9 109.5 reduce-scatter.3
  231.3 45.0 all-gather.2
  328.8 55.2 all-reduce.3
  495.1 108.2 reduce-scatter.5
  735.8 41.2 all-gather.4
  829.5 55.3 all-reduce.5
  995.8 108.3 reduce-scatter.7
where the time goes:
time: 1180 us
  waiting for transfers between devices  525 us (44%)
  other arithmetic  286 us (24%)
  blocking collectives  194 us (16%)
  matrix products  103 us (9%)
  local copies, waits for them, and re-layouts  55.5 us (5%)
  between operations  14.9 us (1%)
    reduce_scatter x3, waiting for transfers between devices, reduce_tiles(): lax.psum_scatter(partial_value, 'orbit', scatter_dimension=0, tiled=True)  327 us
    scatter-add x12, other arithmetic, turn(): jax.ops.segment_sum(contrib, targets, num_segments=tile_count)  229 us
    psum x3, blocking collectives, inner_sum(): lax.psum(jnp.sum(first_vec * second_vec, axis=(0, 1)), ('orbit', 'region'))  194 us
    psum x2, waiting for transfers between devices, per_device(): image = lax.psum(partial_value, 'region')  111 us
    all_gather x2, waiting for transfers between devices, per_device(): lax.all_gather(scaled, 'orbit', axis=0, tiled=True)  87.6 us
    dot_general x12, matrix products, turn(): jnp.einsum('bsc,bsr->bcr', blocks_now, weighted[sound_ids], preferred_ele...  73.4 us
    gather x8, local copies, waits for them, and re-layouts, turn(): whole[tile_ids]  36.8 us
    scatter-add x8, other arithmetic, turn(): jax.ops.segment_sum(products, targets, num_segments=sb_count)  29.7 us
  transfers between devices with their start and end apart: 7, of which 7 were waited for; matrix products, arithmetic and copies ran while one was open for 0% of the time, Pallas kernels for 0%

commit v1 on v0

--- a/solution.py
+++ b/solution.py
@@ -63,7 +63,7 @@
         return lax.psum_scatter(partial_value, "orbit", scatter_dimension=0, tiled=True)
 
     def inner_sum(first_vec, second_vec):
-        return lax.psum(jnp.sum(first_vec * second_vec, axis=(0, 1)), ("orbit", "region"))
+        return lax.psum(lax.psum(jnp.sum(first_vec * second_vec, axis=(0, 1)), "orbit"), "region")
 
     def apply_transpose(weighted):
         return reduce_tiles(

time: 1180 us -> 1210 us (1.025)
  blocking collectives: 194 us -> 217 us
    psum x3 -> x6, blocking collectives: 194 us -> 217 us  [the longest x3 194 us: inner_sum(): lax.psum(jnp.sum(first_vec * second_vec, axis=(0, 1)), 'orbit')]
where the time goes in v1:
time: 1210 us; the launch traced here: 1200 us
  waiting for transfers between devices  525 us (43%)
  other arithmetic  286 us (24%)
  blocking collectives  217 us (18%)
  matrix products  103 us (9%)
  local copies, waits for them, and re-layouts  55.5 us (5%)
  between operations  14.9 us (1%)
    reduce_scatter x3, waiting for transfers between devices, reduce_tiles(): lax.psum_scatter(partial_value, 'orbit', scatter_dimension=0, tiled=True)  327 us
    scatter-add x12, other arithmetic, turn(): jax.ops.segment_sum(contrib, targets, num_segments=tile_count)  229 us
    psum x3, blocking collectives, inner_sum(): lax.psum(jnp.sum(first_vec * second_vec, axis=(0, 1)), 'orbit')  194 us
    psum x2, waiting for transfers between devices, per_device(): image = lax.psum(partial_value, 'region')  111 us
    all_gather x2, waiting for transfers between devices, per_device(): lax.all_gather(scaled, 'orbit', axis=0, tiled=True)  87.5 us
    dot_general x12, matrix products, turn(): jnp.einsum('bsc,bsr->bcr', blocks_now, weighted[sound_ids], preferred_ele...  73.4 us
    gather x8, local copies, waits for them, and re-layouts, turn(): whole[tile_ids]  36.8 us
    scatter-add x8, other arithmetic, turn(): jax.ops.segment_sum(products, targets, num_segments=sb_count)  29.7 us
  transfers between devices with their start and end apart: 7, of which 7 were waited for; matrix products, arithmetic and copies ran while one was open for 0% of the time, Pallas kernels for 0%

profile of v1, /device:TPU:1, one launch (start us, length us, event | category | flops | bytes accessed | tf_op | source)
XLA Modules:
  0.0 1202.0 jit_solution(5460878508863329491)
XLA Ops:
  11.9 106.8 %while.55 = (s32[]{:T(128)}, f32[32,256,128]{2,1,0:T(8,128)}, s32[]{:T(128)}, s32[]{:T(128)}, s32[320]{0:T(512)S(1)}, /*index=5*/bf16[320,64,256]{2,1,0:T(8,128)...) while((s32[]{:T(128)}, f32[32,256,128]{2,1,0:T(8,128)}, ...), condition=%wide.region_2.3_spmd.clone, body=%wide.region_0.2_spmd.clone.sunk | while | flops 270534016 | bytes 38803376 | solution.py:49
  13.4 6.1 fusion.47
  19.5 19.0 %scatter_fusion = f32[32,256,128]{2,1,0:T(8,128)} fusion(f32[32,256,128]{2,1,0:T(8,128)} %get-tuple-element.723, s32[64]{0:T(128)S(1)} %get-tuple-element.668, f32[64,256,128]{2,1,0:T(8,128)} %fusion.47), kind=kCustom, calls=%fused_computation.5.clone.clone.1 | custom fusion | flops 2097152 | bytes 25166080 | tf_op jit(solution)/shard_map/while/body/scatter-add | solution.py:46
  40.1 6.1 fusion.47
  46.2 18.9 %scatter_fusion = f32[32,256,128]{2,1,0:T(8,128)} fusion(f32[32,256,128]{2,1,0:T(8,128)} %get-tuple-element.723, s32[64]{0:T(128)S(1)} %get-tuple-element.668, f32[64,256,128]{2,1,0:T(8,128)} %fusion.47), kind=kCustom, calls=%fused_computation.5.clone.clone.1 | custom fusion | flops 2097152 | bytes 25166080 | tf_op jit(solution)/shard_map/while/body/scatter-add | solution.py:46
  66.6 6.1 fusion.47
  72.7 19.0 %scatter_fusion = f32[32,256,128]{2,1,0:T(8,128)} fusion(f32[32,256,128]{2,1,0:T(8,128)} %get-tuple-element.723, s32[64]{0:T(128)S(1)} %get-tuple-element.668, f32[64,256,128]{2,1,0:T(8,128)} %fusion.47), kind=kCustom, calls=%fused_computation.5.clone.clone.1 | custom fusion | flops 2097152 | bytes 25166080 | tf_op jit(solution)/shard_map/while/body/scatter-add | solution.py:46
  93.2 6.1 fusion.47
  99.3 19.4 %scatter_fusion = f32[32,256,128]{2,1,0:T(8,128)} fusion(f32[32,256,128]{2,1,0:T(8,128)} %get-tuple-element.723, s32[64]{0:T(128)S(1)} %get-tuple-element.668, f32[64,256,128]{2,1,0:T(8,128)} %fusion.47), kind=kCustom, calls=%fused_computation.5.clone.clone.1 | custom fusion | flops 2097152 | bytes 25166080 | tf_op jit(solution)/shard_map/while/body/scatter-add | solution.py:46
  118.8 109.6 %reduce-scatter.4.cloned.1.call-done = f32[1,256,128]{2,1,0:T(8,128)} async-done(((f32[32,256,128]{2,1,0:T(8,128)}), f32[1,256,128]{2,1,0:T(8,128)}) %reduce-scatter.4.cloned.1.call-update) | async-done | bytes 131088 | tf_op jit(solution)/shard_map/reduce_scatter | solution.py:63
  230.2 46.2 %all-gather.3.cloned.1.call-done = bf16[32,256,128]{2,1,0:T(8,128)(2,1)} async-done(((bf16[1,256,128]{2,1,0:T(8,128)(2,1)}), bf16[32,256,128]{2,1,0:T(8,128)(2,1)}) %all-gather.3.cloned.1.call-update) | async-done | bytes 2097168 | tf_op jit(solution)/shard_map/all_gather | solution.py:88
  276.5 51.1 %while.56 = (s32[]{:T(128)}, f32[32,64,128]{2,1,0:T(8,128)S(1)}, s32[]{:T(128)}, s32[]{:T(128)}, s32[320]{0:T(512)S(1)}, /*index=5*/bf16[320,64,256]{2,1,0:T(8,1...) while((s32[]{:T(128)}, f32[32,64,128]{2,1,0:T(8,128)S(1)}, ...), condition=%wide.region_9.10_spmd.clone, body=%wide.region_7.9_spmd.clone.sunk | while | flops 268961152 | bytes 23074740 | solution.py:28
  277.3 4.6 gather_fusion.1
  281.9 3.7 fusion.50
  285.6 3.7 scatter_fusion.1
  290.1 4.6 gather_fusion.1
  294.7 3.7 fusion.50
  298.3 3.7 scatter_fusion.1
  302.8 4.6 gather_fusion.1
  307.4 3.7 fusion.50
  311.1 3.7 scatter_fusion.1
  315.6 4.6 gather_fusion.1
  323.9 3.7 scatter_fusion.1
  328.7 55.4 %all-reduce.5.cloned.1.call-done = f32[32,64,128]{2,1,0:T(8,128)} async-done(((f32[32,64,128]{2,1,0:T(8,128)}), f32[32,64,128]{2,1,0:T(8,128)}) %all-reduce.5.cloned.1.call-update) | async-done | bytes 1048592 | tf_op jit(solution)/shard_map/psum | solution.py:91
  388.2 106.8 %while.57 = (s32[]{:T(128)}, f32[32,256,128]{2,1,0:T(8,128)}, s32[]{:T(128)}, s32[]{:T(128)}, s32[320]{0:T(512)S(1)}, /*index=5*/bf16[320,64,256]{2,1,0:T(8,128)...) while((s32[]{:T(128)}, f32[32,256,128]{2,1,0:T(8,128)}, ...), condition=%wide.region_13.14_spmd.clone, body=%wide.region_11.13_spmd.clone.sunk | while | flops 270534016 | bytes 38803376 | solution.py:49
  389.6 6.1 fusion.53
  395.8 19.0 %scatter_fusion.2 = f32[32,256,128]{2,1,0:T(8,128)} fusion(f32[32,256,128]{2,1,0:T(8,128)} %get-tuple-element.795, s32[64]{0:T(128)S(1)} %get-tuple-element.688, f32[64,256,128]{2,1,0:T(8,128)} %fusion.53), kind=kCustom, calls=%fused_computation.7.clone.clone.1 | custom fusion | flops 2097152 | bytes 25166080 | tf_op jit(solution)/shard_map/while/body/scatter-add | solution.py:46
  416.3 6.1 fusion.53
  422.4 18.9 %scatter_fusion.2 = f32[32,256,128]{2,1,0:T(8,128)} fusion(f32[32,256,128]{2,1,0:T(8,128)} %get-tuple-element.795, s32[64]{0:T(128)S(1)} %get-tuple-element.688, f32[64,256,128]{2,1,0:T(8,128)} %fusion.53), kind=kCustom, calls=%fused_computation.7.clone.clone.1 | custom fusion | flops 2097152 | bytes 25166080 | tf_op jit(solution)/shard_map/while/body/scatter-add | solution.py:46
  442.8 6.1 fusion.53
  448.9 19.0 %scatter_fusion.2 = f32[32,256,128]{2,1,0:T(8,128)} fusion(f32[32,256,128]{2,1,0:T(8,128)} %get-tuple-element.795, s32[64]{0:T(128)S(1)} %get-tuple-element.688, f32[64,256,128]{2,1,0:T(8,128)} %fusion.53), kind=kCustom, calls=%fused_computation.7.clone.clone.1 | custom fusion | flops 2097152 | bytes 25166080 | tf_op jit(solution)/shard_map/while/body/scatter-add | solution.py:46
  469.4 6.1 fusion.53
  475.5 19.4 %scatter_fusion.2 = f32[32,256,128]{2,1,0:T(8,128)} fusion(f32[32,256,128]{2,1,0:T(8,128)} %get-tuple-element.795, s32[64]{0:T(128)S(1)} %get-tuple-element.688, f32[64,256,128]{2,1,0:T(8,128)} %fusion.53), kind=kCustom, calls=%fused_computation.7.clone.clone.1 | custom fusion | flops 2097152 | bytes 25166080 | tf_op jit(solution)/shard_map/while/body/scatter-add | solution.py:46
  495.0 108.4 %reduce-scatter.6.cloned.1.call-done = f32[1,256,128]{2,1,0:T(8,128)} async-done(((f32[32,256,128]{2,1,0:T(8,128)}), f32[1,256,128]{2,1,0:T(8,128)}) %reduce-scatter.6.cloned.1.call-update) | async-done | bytes 131088 | tf_op jit(solution)/shard_map/reduce_scatter | solution.py:63
  604.4 64.4 %all-reduce = (f32[128]{0:T(128)S(1)}, f32[128]{0:T(128)S(1)}) all-reduce(f32[128]{0:T(128)S(1)} %get-tuple-element.343, f32[128]{0:T(128)S(1)} %get-tuple-element.342), channel_id=1, replica_groups=mesh['orbit'=32,'region'=4] {'orbit'}, use_global_device_ids=true, to_apply=%region_5.6 | all-reduce | flops 256 | bytes 2048 | tf_op jit(solution)/shard_map/psum | solution.py:66
  668.8 8.4 all-reduce.1
  678.3 65.1 %psum.75 = f32[128]{0:T(128)S(1)} all-reduce(f32[128]{0:T(128)S(1)} %multiply_reduce_fusion.1), channel_id=1, replica_groups=mesh['orbit'=32,'region'=4] {'orbit'}, use_global_device_ids=true, to_apply=%region_19.20 | all-reduce | flops 128 | bytes 1024 | tf_op jit(solution)/shard_map/psum | solution.py:66
  743.3 6.0 psum.76
  751.1 41.2 %all-gather.5.cloned.1.call-done = bf16[32,256,128]{2,1,0:T(8,128)(2,1)} async-done(((bf16[1,256,128]{2,1,0:T(8,128)(2,1)}), bf16[32,256,128]{2,1,0:T(8,128)(2,1)}) %all-gather.5.cloned.1.call-update) | async-done | bytes 2097168 | tf_op jit(solution)/shard_map/all_gather | solution.py:88
  792.4 51.3 %while.58 = (s32[]{:T(128)}, f32[32,64,128]{2,1,0:T(8,128)S(1)}, s32[]{:T(128)}, s32[]{:T(128)}, s32[320]{0:T(512)S(1)}, /*index=5*/bf16[320,64,256]{2,1,0:T(8,1...) while((s32[]{:T(128)}, f32[32,64,128]{2,1,0:T(8,128)S(1)}, ...), condition=%wide.region_23.24_spmd.clone, body=%wide.region_21.23_spmd.clone.sunk | while | flops 268961152 | bytes 23074740 | solution.py:28
  793.3 4.6 gather_fusion.3
  797.9 3.7 fusion.56
  801.6 3.7 scatter_fusion.3
  806.1 4.6 gather_fusion.3
  810.7 3.7 fusion.56
  814.4 3.7 scatter_fusion.3
  818.9 4.6 gather_fusion.3
  823.5 3.7 fusion.56
  827.2 3.7 scatter_fusion.3
  831.6 4.6 gather_fusion.3
  839.9 3.7 scatter_fusion.3
  844.8 55.4 %all-reduce.7.cloned.1.call-done = f32[32,64,128]{2,1,0:T(8,128)} async-done(((f32[32,64,128]{2,1,0:T(8,128)}), f32[32,64,128]{2,1,0:T(8,128)}) %all-reduce.7.cloned.1.call-update) | async-done | bytes 1048592 | tf_op jit(solution)/shard_map/psum | solution.py:91
  904.2 106.8 %while.59 = (s32[]{:T(128)}, f32[32,256,128]{2,1,0:T(8,128)}, s32[]{:T(128)}, s32[]{:T(128)}, s32[320]{0:T(512)S(1)}, /*index=5*/bf16[320,64,256]{2,1,0:T(8,128)...) while((s32[]{:T(128)}, f32[32,256,128]{2,1,0:T(8,128)}, ...), condition=%wide.region_27.28_spmd.clone, body=%wide.region_25.27_spmd.clone.sunk | while | flops 270534016 | bytes 38803376 | solution.py:49
  905.7 6.1 fusion.59
  911.8 19.0 %scatter_fusion.4 = f32[32,256,128]{2,1,0:T(8,128)} fusion(f32[32,256,128]{2,1,0:T(8,128)} %get-tuple-element.867, s32[64]{0:T(128)S(1)} %get-tuple-element.708, f32[64,256,128]{2,1,0:T(8,128)} %fusion.59), kind=kCustom, calls=%fused_computation.9.clone.clone.1 | custom fusion | flops 2097152 | bytes 25166080 | tf_op jit(solution)/shard_map/while/body/scatter-add | solution.py:46
  932.3 6.1 fusion.59
  938.5 18.9 %scatter_fusion.4 = f32[32,256,128]{2,1,0:T(8,128)} fusion(f32[32,256,128]{2,1,0:T(8,128)} %get-tuple-element.867, s32[64]{0:T(128)S(1)} %get-tuple-element.708, f32[64,256,128]{2,1,0:T(8,128)} %fusion.59), kind=kCustom, calls=%fused_computation.9.clone.clone.1 | custom fusion | flops 2097152 | bytes 25166080 | tf_op jit(solution)/shard_map/while/body/scatter-add | solution.py:46
  958.8 6.1 fusion.59
  965.0 19.0 %scatter_fusion.4 = f32[32,256,128]{2,1,0:T(8,128)} fusion(f32[32,256,128]{2,1,0:T(8,128)} %get-tuple-element.867, s32[64]{0:T(128)S(1)} %get-tuple-element.708, f32[64,256,128]{2,1,0:T(8,128)} %fusion.59), kind=kCustom, calls=%fused_computation.9.clone.clone.1 | custom fusion | flops 2097152 | bytes 25166080 | tf_op jit(solution)/shard_map/while/body/scatter-add | solution.py:46
  985.5 6.1 fusion.59
  991.6 19.4 %scatter_fusion.4 = f32[32,256,128]{2,1,0:T(8,128)} fusion(f32[32,256,128]{2,1,0:T(8,128)} %get-tuple-element.867, s32[64]{0:T(128)S(1)} %get-tuple-element.708, f32[64,256,128]{2,1,0:T(8,128)} %fusion.59), kind=kCustom, calls=%fused_computation.9.clone.clone.1 | custom fusion | flops 2097152 | bytes 25166080 | tf_op jit(solution)/shard_map/while/body/scatter-add | solution.py:46
  1011.0 108.5 %reduce-scatter.8.cloned.1.call-done = f32[1,256,128]{2,1,0:T(8,128)} async-done(((f32[32,256,128]{2,1,0:T(8,128)}), f32[1,256,128]{2,1,0:T(8,128)}) %reduce-scatter.8.cloned.1.call-update) | async-done | bytes 131088 | tf_op jit(solution)/shard_map/reduce_scatter | solution.py:63
  1120.6 64.3 %psum.78 = f32[128]{0:T(128)S(1)} all-reduce(f32[128]{0:T(128)S(1)} %multiply_reduce_fusion), channel_id=1, replica_groups=mesh['orbit'=32,'region'=4] {'orbit'}, use_global_device_ids=true, to_apply=%region_30.31 | all-reduce | flops 128 | bytes 1024 | tf_op jit(solution)/shard_map/psum | solution.py:66
  1185.0 8.4 psum.79
  (101 shorter events, 53.8 us)
Async XLA Ops:
  7.2 4.8 copy-start.6
  7.2 4.8 copy-start.5
  7.2 221.3 %reduce-scatter.4.cloned.1.call-start = ((), (), s32[]{:S(2)}) async-start(), calls=%async_computation.3 | async-start | bytes 4325376 | tf_op jit(solution)/shard_map/reduce_scatter | solution.py:63
  118.7 109.7 %copy-start.7 = (f32[1,1,256]{2,1,0:T(1,128)S(1)}, f32[1,1,256]{2,1,0:T(1,128)}, u32[]{:S(2)}) copy-start(f32[1,1,256]{2,1,0:T(1,128)} %param.23) | copy-start | bytes 3076
  118.7 157.7 %all-gather.3.cloned.1.call-start = ((), (), s32[]{:S(2)}) async-start(), calls=%async_computation.4 | async-start | bytes 2162688 | tf_op jit(solution)/shard_map/all_gather | solution.py:88
  230.1 154.0 %all-reduce.5.cloned.1.call-start = ((), (), s32[]{:S(2)}) async-start(), calls=%async_computation.5 | async-start | bytes 2097152 | tf_op jit(solution)/shard_map/psum | solution.py:91
  276.5 107.6 %copy-start.4 = (f32[32,64]{1,0:T(8,128)S(1)}, f32[32,64]{1,0:T(8,128)}, u32[]{:S(2)}) copy-start(f32[32,64]{1,0:T(8,128)} %param.22) | copy-start | bytes 24580
  327.6 1.0 copy-start
  328.7 274.7 %reduce-scatter.6.cloned.1.call-start = ((), (), s32[]{:S(2)}) async-start(), calls=%async_computation.6 | async-start | bytes 4325376 | tf_op jit(solution)/shard_map/reduce_scatter | solution.py:63
  495.0 108.5 %copy-start.2 = (f32[1,256,128]{2,1,0:T(8,128)S(1)}, f32[1,256,128]{2,1,0:T(8,128)}, u32[]{:S(2)}) copy-start(f32[1,256,128]{2,1,0:T(8,128)} %reduce-scatter.4.cloned.1.call-done) | copy-start | bytes 393220
  495.0 297.3 %all-gather.5.cloned.1.call-start = ((), (), s32[]{:S(2)}) async-start(), calls=%async_computation.7 | async-start | bytes 2162688 | tf_op jit(solution)/shard_map/all_gather | solution.py:88
  751.0 149.2 %all-reduce.7.cloned.1.call-start = ((), (), s32[]{:S(2)}) async-start(), calls=%async_computation.8 | async-start | bytes 2097152 | tf_op jit(solution)/shard_map/psum | solution.py:91
  843.7 1.0 copy-start.1
  844.7 274.8 %reduce-scatter.8.cloned.1.call-start = ((), (), s32[]{:S(2)}) async-start(), calls=%async_computation.9 | async-start | bytes 4325376 | tf_op jit(solution)/shard_map/reduce_scatter | solution.py:63
  1011.0 108.6 %copy-start.3 = (f32[1,256,128]{2,1,0:T(8,128)S(1)}, f32[1,256,128]{2,1,0:T(8,128)}, u32[]{:S(2)}) copy-start(f32[1,256,128]{2,1,0:T(8,128)} %reduce-scatter.6.cloned.1.call-done) | copy-start | bytes 393220
Sparse Core Ops, SparseCore 0:
  118.9 109.5 reduce-scatter.3
  231.3 45.0 all-gather.2
  328.8 55.2 all-reduce.4
  495.1 108.2 reduce-scatter.5
  751.1 41.1 all-gather.4
  844.8 55.2 all-reduce.6
  1011.1 108.3 reduce-scatter.7
